TPU v7x, 512 devices: a whole 4x4x16 slice. The times are simulated.
512 devices in a mesh: blk: 64 (over y, z_lo, core), group: 8 (over x, z_hi).
Axes of the slice: x: 4, y: 4, z: 16 (z_hi: 2, z_lo: 8; z = z_hi * 8 + z_lo), core: 2. Of those that a mesh axis runs over, the one named last changes fastest.
Arguments:
- audio_embed: float32 [49152, 512], P('blk'), may hold values from -4 to 4
- text_embed: float32 [49152, 512], P(('blk', 'group')), may hold values from -4 to 4
Outputs:
- grad_audio: float32 [49152, 512], P(('blk', 'group'))
- grad_text: float32 [49152, 512], P(('blk', 'group'))
- loss_rows: float32 [49152], P(('blk', 'group'))
- loss_cols: float32 [49152], P(('blk', 'group'))
All inputs are finite; a program needn't handle non-finite values.
Results may differ from a plain program's by a relative error of at most 0.0003.
Values sent between devices are 32-bit elements; how exact they have to be, the bound alone decides.
No kernel may reach another device: no remote copies, remote signals or barrier semaphores. Data moves between devices by JAX's collectives and lax.ppermute only.
A program may use at most 64 MiB of HBM per device.

v0:
```python
import jax
import jax.numpy as jnp
from jax import lax
from jax.sharding import PartitionSpec as P

SPAN = 3
logit_scale = 1.0 / 0.07
precise = lax.Precision.HIGHEST


def shifted(value, axis, by):
    devices = lax.axis_size(axis)
    return lax.ppermute(value, axis, [(i, (i + by) % devices) for i in range(devices)])


def send_ahead(payload):
    return shifted(payload, "blk", -1)


def send_back(payload):
    return shifted(payload, "blk", 1)


def pair_merge(earlier, later):
    highest = jnp.maximum(earlier[0], later[0])
    return (
        highest,
        earlier[1] * jnp.exp(earlier[0] - highest) + later[1] * jnp.exp(later[0] - highest),
    )


def shards(audio_embed, text_embed):
    row_count = audio_embed.shape[0]
    text_rows = text_embed.shape[0]
    member = lax.axis_index("group")
    text_tiles = [text_embed]
    moving = text_embed
    for _ in range(SPAN - 1):
        moving = send_ahead(moving)
        text_tiles.append(moving)
    window = jnp.stack(text_tiles)
    logits = logit_scale * jnp.einsum("rd,kcd->rkc", audio_embed, window, precision=precise)
    local_max = jnp.max(logits, axis=(1, 2))
    row_max = lax.pmax(local_max, "group")
    row_total = lax.psum(jnp.sum(jnp.exp(logits - row_max[:, None, None]), axis=(1, 2)), "group")
    row_lse = row_max + jnp.log(row_total)
    col_max = jnp.max(logits, axis=0)
    col_sum = jnp.sum(jnp.exp(logits - col_max[None]), axis=0)
    carried = (col_max[SPAN - 1], col_sum[SPAN - 1])
    for offset in range(SPAN - 2, -1, -1):
        arrived = send_back(carried)
        carried = pair_merge(arrived, (col_max[offset], col_sum[offset]))
    col_lse = carried[0] + jnp.log(carried[1])
    lse_tiles = [col_lse]
    moving = col_lse
    for _ in range(SPAN - 1):
        moving = send_ahead(moving)
        lse_tiles.append(moving)
    lse_window = jnp.stack(lse_tiles)
    soft_weights = 0.5 * (
        jnp.exp(logits - row_lse[:, None, None]) + jnp.exp(logits - lse_window[None])
    )
    row_ids = lax.broadcasted_iota(jnp.int32, (row_count, SPAN, text_rows), 0)
    tile_ids = lax.broadcasted_iota(jnp.int32, (row_count, SPAN, text_rows), 1)
    col_ids = lax.broadcasted_iota(jnp.int32, (row_count, SPAN, text_rows), 2)
    positive = ((tile_ids == 0) & (row_ids == member * text_rows + col_ids)).astype(jnp.float32)
    grad_logits = soft_weights - positive
    text_parts = logit_scale * jnp.einsum(
        "rkc,rd->kcd", grad_logits, audio_embed, precision=precise
    )
    grad_sum = text_parts[SPAN - 1]
    for offset in range(SPAN - 2, -1, -1):
        grad_sum = send_back(grad_sum) + text_parts[offset]
    own_logits = lax.dynamic_slice_in_dim(logits[:, 0, :], member * text_rows, text_rows, 0)
    positive_scores = jnp.diagonal(own_logits)
    own_lse = lax.dynamic_slice_in_dim(row_lse, member * text_rows, text_rows, 0)
    loss_rows = own_lse - positive_scores
    loss_cols = col_lse - positive_scores
    grad_audio = lax.psum_scatter(
        logit_scale * jnp.einsum("rkc,kcd->rd", grad_logits, window, precision=precise),
        "group",
        scatter_dimension=0,
        tiled=True,
    )
    return (grad_audio, grad_sum, loss_rows, loss_cols)


def solution(mesh):
    placed = (P("blk", None), P(("blk", "group"), None))
    return jax.shard_map(
        shards,
        mesh=mesh,
        in_specs=placed,
        out_specs=(
            P(("blk", "group"), None),
            P(("blk", "group"), None),
            P(("blk", "group")),
            P(("blk", "group")),
        ),
        check_vma=False,
    )
```

profile of v0, /device:TPU:8, one launch (start us, length us, event | category | flops | bytes accessed | tf_op | source)
XLA Modules:
  0.0 297.5 jit_solution(14635427026608289326)
XLA Ops:
  7.2 0.0 copy-start
  7.2 0.0 reduce-scatter.2.cloned.1.call-start
  7.2 12.6 %collective-permute-start = (f32[96,512]{1,0:T(8,128)}, f32[96,512]{1,0:T(8,128)S(1)}, u32[]{:S(2)}, u32[]{:S(2)}) collective-permute-start(f32[96,512]{1,0:T(8,128)} %param.3), channel_id=1, source_target_pairs={{0,504},{8,0},{16,8},{24,16},{32,24},{40,32},{48,40},{56,48},{64,5... | collective-permute-start | bytes 589832 | tf_op jit(solution)/shard_map/ppermute | solution.py:13
  19.8 3.5 %collective-permute-done = f32[96,512]{1,0:T(8,128)S(1)} collective-permute-done((f32[96,512]{1,0:T(8,128)}, f32[96,512]{1,0:T(8,128)S(1)}, u32[]{:S(2)}, u32[]{:S(2)}) %collective-permute-start) | collective-permute-done | bytes 196640 | tf_op jit(solution)/shard_map/ppermute | solution.py:13
  23.3 11.2 %collective-permute-start.1 = (f32[96,512]{1,0:T(8,128)S(1)}, f32[96,512]{1,0:T(8,128)S(1)}, u32[]{:S(2)}, u32[]{:S(2)}) collective-permute-start(f32[96,512]{1,0:T(8,128)S(1)} %collective-permute-done), channel_id=1, source_target_pairs={{0,504},{8,0},{16,8},{24,16},{32,24},{40,32},{48,40},{56,48},{64,5... | collective-permute-start | bytes 589832 | tf_op jit(solution)/shard_map/ppermute | solution.py:13
  34.6 3.2 %collective-permute-done.1 = f32[96,512]{1,0:T(8,128)S(1)} collective-permute-done((f32[96,512]{1,0:T(8,128)S(1)}, f32[96,512]{1,0:T(8,128)S(1)}, u32[]{:S(2)}, u32[]{:S(2)}) %collective-permute-start.1) | collective-permute-done | bytes 196640 | tf_op jit(solution)/shard_map/ppermute | solution.py:13
  37.8 0.0 copy-done
  37.8 2.6 fusion.26
  40.4 0.0 copy-start.1
  40.4 42.0 %pmax.7 = f32[768]{0:T(1024)S(1)} all-reduce(f32[768]{0:T(1024)S(1)} %get-tuple-element.11), channel_id=1, replica_groups=mesh['blk'=64,'group'=8] {'group'}, use_global_device_ids=true, to_apply=%region_1.0 | all-reduce | flops 768 | bytes 6144 | tf_op jit(solution)/shard_map/pmax | solution.py:44
  82.4 0.2 exponential_reduce_fusion.1
  82.6 0.3 exponential_reduce_fusion
  83.0 1.9 collective-permute-start.2
  84.9 1.9 collective-permute-start.4
  86.8 35.9 %psum.7 = f32[768]{0:T(1024)S(1)} all-reduce(f32[768]{0:T(1024)S(1)} %get-tuple-element.4), channel_id=1, replica_groups=mesh['blk'=64,'group'=8] {'group'}, use_global_device_ids=true, to_apply=%region_3.0 | all-reduce | flops 768 | bytes 6144 | tf_op jit(solution)/shard_map/psum | solution.py:45
  122.7 0.0 collective-permute-done.2
  122.7 0.0 collective-permute-done.4
  122.8 1.9 collective-permute-start.5
  124.7 1.9 collective-permute-start.3
  126.6 0.1 dynamic-slice_bitcast_fusion
  126.7 1.3 gather_fusion
  128.0 7.2 %collective-permute-done.5 = f32[96]{0:T(128)S(1)} collective-permute-done((f32[96]{0:T(128)S(1)}, f32[96]{0:T(128)S(1)}, u32[]{:S(2)}, u32[]{:S(2)}) %collective-permute-start.5) | collective-permute-done | bytes 416 | tf_op jit(solution)/shard_map/ppermute | solution.py:13
  135.2 1.9 collective-permute-done.3
  137.1 0.6 fusion.24
  137.7 2.1 collective-permute-start.6
  139.8 1.3 collective-permute-done.6
  141.0 11.1 %collective-permute-start.7 = (f32[96]{0:T(128)S(1)}, f32[96]{0:T(128)S(1)}, u32[]{:S(2)}, u32[]{:S(2)}) collective-permute-start(f32[96]{0:T(128)S(1)} %collective-permute-done.6), channel_id=1, source_target_pairs={{0,504},{8,0},{16,8},{24,16},{32,24},{40,32},{48,40},{56,48},{64,5... | collective-permute-start | bytes 1160 | tf_op jit(solution)/shard_map/ppermute | solution.py:13
  152.2 1.3 collective-permute-done.7
  153.4 0.0 copy-done.1
  153.4 4.2 %bitcast_multiply_fusion = f32[768,512]{1,0:T(8,128)} fusion(f32[1,96,512]{2,1,0:T(8,128)S(1)} %bitcast.90, f32[1,96,512]{2,1,0:T(8,128)S(1)} %bitcast.88, f32[1,96,512]{2,1,0:T(8,128)S(1)} %bitcast.86, s32[96]{0:T(128)S(1)} %iota_add_fusion, f32[3,96]{1,0:T(4,128)S(1)} %pad_maximum_fusion.3, f32[768]{0:T(1024)S(1)} %log_add_fusion, ...), kind=kOutput, calls=%fused_computation.1 | convolution fusion | flops 1361412096 | bytes 3052035 | tf_op jit(solution)/shard_map/rkc,kcd->rd/dot_general | solution.py:80
  157.6 0.0 reduce-scatter.2.cloned.1.call-update
  157.6 2.0 fusion.7
  159.7 1.9 collective-permute-start.8
  161.6 12.6 %collective-permute-done.8 = f32[96,512]{1,0:T(8,128)S(1)} collective-permute-done((f32[96,512]{1,0:T(8,128)S(1)}, f32[96,512]{1,0:T(8,128)S(1)}, u32[]{:S(2)}, u32[]{:S(2)}) %collective-permute-start.8) | collective-permute-done | bytes 196640 | tf_op jit(solution)/shard_map/ppermute | solution.py:13
  174.2 1.9 collective-permute-start.9
  176.1 20.8 %collective-permute-done.9 = f32[96,512]{1,0:T(8,128)S(1)} collective-permute-done((f32[96,512]{1,0:T(8,128)S(1)}, f32[96,512]{1,0:T(8,128)S(1)}, u32[]{:S(2)}, u32[]{:S(2)}) %collective-permute-start.9) | collective-permute-done | bytes 196640 | tf_op jit(solution)/shard_map/ppermute | solution.py:13
  196.9 0.7 fusion.11
  197.7 93.0 %reduce-scatter.2.cloned.1.call-done = f32[96,512]{1,0:T(8,128)} async-done(((f32[768,512]{1,0:T(8,128)}), f32[96,512]{1,0:T(8,128)}) %reduce-scatter.2.cloned.1.call-update) | async-done | bytes 196624 | tf_op jit(solution)/shard_map/reduce_scatter | solution.py:79
  (11 shorter events, 0.1 us)
Async XLA Ops:
  7.2 30.6 %copy-start = (f32[768,512]{1,0:T(8,128)S(1)}, f32[768,512]{1,0:T(8,128)}, u32[]{:S(2)}) copy-start(f32[768,512]{1,0:T(8,128)} %param.2) | copy-start | bytes 4718596
  7.2 283.5 %reduce-scatter.2.cloned.1.call-start = ((), (), s32[]{:S(2)}) async-start(), calls=%async_computation.1 | async-start | bytes 1769472 | tf_op jit(solution)/shard_map/reduce_scatter | solution.py:79
  7.2 16.1 %collective-permute-start = (f32[96,512]{1,0:T(8,128)}, f32[96,512]{1,0:T(8,128)S(1)}, u32[]{:S(2)}, u32[]{:S(2)}) collective-permute-start(f32[96,512]{1,0:T(8,128)} %param.3), channel_id=1, source_target_pairs={{0,504},{8,0},{16,8},{24,16},{32,24},{40,32},{48,40},{56,48},{64,5... | collective-permute-start | bytes 589832 | tf_op jit(solution)/shard_map/ppermute | solution.py:13
  23.3 14.4 %collective-permute-start.1 = (f32[96,512]{1,0:T(8,128)S(1)}, f32[96,512]{1,0:T(8,128)S(1)}, u32[]{:S(2)}, u32[]{:S(2)}) collective-permute-start(f32[96,512]{1,0:T(8,128)S(1)} %collective-permute-done), channel_id=1, source_target_pairs={{0,504},{8,0},{16,8},{24,16},{32,24},{40,32},{48,40},{56,48},{64,5... | collective-permute-start | bytes 589832 | tf_op jit(solution)/shard_map/ppermute | solution.py:13
  40.4 113.1 %copy-start.1 = (f32[96,512]{1,0:T(8,128)S(1)}, f32[96,512]{1,0:T(8,128)}, u32[]{:S(2)}) copy-start(f32[96,512]{1,0:T(8,128)} %param.3) | copy-start | bytes 589828
  83.0 39.8 %collective-permute-start.2 = (f32[96]{0:T(128)S(1)}, f32[96]{0:T(128)S(1)}, u32[]{:S(2)}, u32[]{:S(2)}) collective-permute-start(f32[96]{0:T(128)S(1)} %slice_bitcast_fusion.4), channel_id=1, source_target_pairs={{0,8},{8,16},{16,24},{24,32},{32,40},{40,48},{48,56},{56,64},{64,7... | collective-permute-start | bytes 1160 | tf_op jit(solution)/shard_map/ppermute | solution.py:13
  84.9 37.8 %collective-permute-start.4 = (f32[96]{0:T(128)S(1)}, f32[96]{0:T(128)S(1)}, u32[]{:S(2)}, u32[]{:S(2)}) collective-permute-start(f32[96]{0:T(128)S(1)} %slice_bitcast_fusion.3), channel_id=1, source_target_pairs={{0,8},{8,16},{16,24},{24,32},{32,40},{40,48},{48,56},{56,64},{64,7... | collective-permute-start | bytes 1160 | tf_op jit(solution)/shard_map/ppermute | solution.py:13
  122.8 12.4 %collective-permute-start.5 = (f32[96]{0:T(128)S(1)}, f32[96]{0:T(128)S(1)}, u32[]{:S(2)}, u32[]{:S(2)}) collective-permute-start(f32[96]{0:T(128)S(1)} %get-tuple-element.9), channel_id=1, source_target_pairs={{0,8},{8,16},{16,24},{24,32},{32,40},{40,48},{48,56},{56,64},{64,7... | collective-permute-start | bytes 1160 | tf_op jit(solution)/shard_map/ppermute | solution.py:13
  124.7 12.4 %collective-permute-start.3 = (f32[96]{0:T(128)S(1)}, f32[96]{0:T(128)S(1)}, u32[]{:S(2)}, u32[]{:S(2)}) collective-permute-start(f32[96]{0:T(128)S(1)} %get-tuple-element.8), channel_id=1, source_target_pairs={{0,8},{8,16},{16,24},{24,32},{32,40},{40,48},{48,56},{56,64},{64,7... | collective-permute-start | bytes 1160 | tf_op jit(solution)/shard_map/ppermute | solution.py:13
  137.7 3.4 %collective-permute-start.6 = (f32[96]{0:T(128)S(1)}, f32[96]{0:T(128)S(1)}, u32[]{:S(2)}, u32[]{:S(2)}) collective-permute-start(f32[96]{0:T(128)S(1)} %get-tuple-element.7), channel_id=1, source_target_pairs={{0,504},{8,0},{16,8},{24,16},{32,24},{40,32},{48,40},{56,48},{64,5... | collective-permute-start | bytes 1160 | tf_op jit(solution)/shard_map/ppermute | solution.py:13
  141.0 12.4 %collective-permute-start.7 = (f32[96]{0:T(128)S(1)}, f32[96]{0:T(128)S(1)}, u32[]{:S(2)}, u32[]{:S(2)}) collective-permute-start(f32[96]{0:T(128)S(1)} %collective-permute-done.6), channel_id=1, source_target_pairs={{0,504},{8,0},{16,8},{24,16},{32,24},{40,32},{48,40},{56,48},{64,5... | collective-permute-start | bytes 1160 | tf_op jit(solution)/shard_map/ppermute | solution.py:13
  159.7 14.5 %collective-permute-start.8 = (f32[96,512]{1,0:T(8,128)S(1)}, f32[96,512]{1,0:T(8,128)S(1)}, u32[]{:S(2)}, u32[]{:S(2)}) collective-permute-start(f32[96,512]{1,0:T(8,128)S(1)} %slice_bitcast_fusion.2), channel_id=1, source_target_pairs={{0,8},{8,16},{16,24},{24,32},{32,40},{40,48},{48,56},{56,64},{64,7... | collective-permute-start | bytes 589832 | tf_op jit(solution)/shard_map/ppermute | solution.py:13
  174.2 22.8 %collective-permute-start.9 = (f32[96,512]{1,0:T(8,128)S(1)}, f32[96,512]{1,0:T(8,128)S(1)}, u32[]{:S(2)}, u32[]{:S(2)}) collective-permute-start(f32[96,512]{1,0:T(8,128)S(1)} %fusion.12), channel_id=1, source_target_pairs={{0,8},{8,16},{16,24},{24,32},{32,40},{40,48},{48,56},{56,64},{64,7... | collective-permute-start | bytes 589832 | tf_op jit(solution)/shard_map/ppermute | solution.py:13
Sparse Core Ops, SparseCore 0:
  157.8 132.8 reduce-scatter.1
where the time goes:
time: 298 us; the launch traced here: 297 us
  waiting for transfers between devices  145 us (49%)
  blocking collectives  77.9 us (26%)
  starting transfers between devices  48.6 us (16%)
  between operations  14.2 us (5%)
  matrix products  8.73 us (3%)
    reduce_scatter x1, waiting for transfers between devices, shards(): lax.psum_scatter(logit_scale * jnp.einsum('rkc,kcd->rd', grad_logits, win...  93 us
    ppermute x10, waiting for transfers between devices, shifted(): lax.ppermute(value, axis, [(i, (i + by) % devices) for i in range(devices)])  51.7 us
    ppermute x10, starting transfers between devices, shifted(): lax.ppermute(value, axis, [(i, (i + by) % devices) for i in range(devices)])  48.5 us
    pmax x1, blocking collectives, shards(): row_max = lax.pmax(local_max, 'group')  42 us
    psum x1, blocking collectives, shards(): lax.psum(jnp.sum(jnp.exp(logits - row_max[:, None, None]), axis=(1, 2)),...  35.9 us
  transfers between devices with their start and end apart: 11, of which 9 were waited for; matrix products, arithmetic and copies ran while one was open for 1% of the time, Pallas kernels for 0%

commit v1 on v0

--- a/solution.py
+++ b/solution.py
@@ -42,7 +42,10 @@
     logits = logit_scale * jnp.einsum("rd,kcd->rkc", audio_embed, window, precision=precise)
     local_max = jnp.max(logits, axis=(1, 2))
     row_max = lax.pmax(local_max, "group")
-    row_total = lax.psum(jnp.sum(jnp.exp(logits - row_max[:, None, None]), axis=(1, 2)), "group")
+    row_total = jnp.sum(
+        lax.all_gather(jnp.sum(jnp.exp(logits - row_max[:, None, None]), axis=(1, 2)), "group"),
+        axis=0,
+    )
     row_lse = row_max + jnp.log(row_total)
     col_max = jnp.max(logits, axis=0)
     col_sum = jnp.sum(jnp.exp(logits - col_max[None]), axis=0)

time: 298 us -> 325 us (1.091)
  blocking collectives: 77.9 us -> 105 us
    all_gather x0 -> x1, blocking collectives: none -> 63.1 us  [shards(): lax.all_gather(jnp.sum(jnp.exp(logits - row_max[:, None, None]), axis=(1,...]
    psum x1 -> x0, blocking collectives: 35.9 us -> none  [shards(): lax.psum(jnp.sum(jnp.exp(logits - row_max[:, None, None]), axis=(1, 2)),...]
where the time goes in v1:
time: 325 us
  waiting for transfers between devices  145 us (45%)
  blocking collectives  105 us (32%)
  starting transfers between devices  48.6 us (15%)
  between operations  14.2 us (4%)
  matrix products  8.73 us (3%)
    reduce_scatter x1, waiting for transfers between devices, shards(): lax.psum_scatter(logit_scale * jnp.einsum('rkc,kcd->rd', grad_logits, win...  93.3 us
    all_gather x1, blocking collectives, shards(): lax.all_gather(jnp.sum(jnp.exp(logits - row_max[:, None, None]), axis=(1,...  63.1 us
    ppermute x10, waiting for transfers between devices, shifted(): lax.ppermute(value, axis, [(i, (i + by) % devices) for i in range(devices)])  51.5 us
    ppermute x10, starting transfers between devices, shifted(): lax.ppermute(value, axis, [(i, (i + by) % devices) for i in range(devices)])  48.5 us
    pmax x1, blocking collectives, shards(): row_max = lax.pmax(local_max, 'group')  41.9 us
  transfers between devices with their start and end apart: 11, of which 9 were waited for; matrix products, arithmetic and copies ran while one was open for 1% of the time, Pallas kernels for 0%

profile of v1, /device:TPU:8, one launch (start us, length us, event | category | flops | bytes accessed | tf_op | source)
XLA Modules:
  0.0 324.6 jit_solution(7437538481984118051)
XLA Ops:
  7.2 0.0 copy-start
  7.2 0.0 reduce-scatter.2.cloned.1.call-start
  7.2 12.6 %collective-permute-start = (f32[96,512]{1,0:T(8,128)}, f32[96,512]{1,0:T(8,128)S(1)}, u32[]{:S(2)}, u32[]{:S(2)}) collective-permute-start(f32[96,512]{1,0:T(8,128)} %param.3), channel_id=1, source_target_pairs={{0,504},{8,0},{16,8},{24,16},{32,24},{40,32},{48,40},{56,48},{64,5... | collective-permute-start | bytes 589832 | tf_op jit(solution)/shard_map/ppermute | solution.py:13
  19.8 3.5 %collective-permute-done = f32[96,512]{1,0:T(8,128)S(1)} collective-permute-done((f32[96,512]{1,0:T(8,128)}, f32[96,512]{1,0:T(8,128)S(1)}, u32[]{:S(2)}, u32[]{:S(2)}) %collective-permute-start) | collective-permute-done | bytes 196640 | tf_op jit(solution)/shard_map/ppermute | solution.py:13
  23.3 11.2 %collective-permute-start.1 = (f32[96,512]{1,0:T(8,128)S(1)}, f32[96,512]{1,0:T(8,128)S(1)}, u32[]{:S(2)}, u32[]{:S(2)}) collective-permute-start(f32[96,512]{1,0:T(8,128)S(1)} %collective-permute-done), channel_id=1, source_target_pairs={{0,504},{8,0},{16,8},{24,16},{32,24},{40,32},{48,40},{56,48},{64,5... | collective-permute-start | bytes 589832 | tf_op jit(solution)/shard_map/ppermute | solution.py:13
  34.6 3.3 %collective-permute-done.1 = f32[96,512]{1,0:T(8,128)S(1)} collective-permute-done((f32[96,512]{1,0:T(8,128)S(1)}, f32[96,512]{1,0:T(8,128)S(1)}, u32[]{:S(2)}, u32[]{:S(2)}) %collective-permute-start.1) | collective-permute-done | bytes 196640 | tf_op jit(solution)/shard_map/ppermute | solution.py:13
  37.8 0.0 copy-done
  37.8 2.6 fusion.26
  40.4 41.9 %pmax.7 = f32[768]{0:T(1024)S(1)} all-reduce(f32[768]{0:T(1024)S(1)} %get-tuple-element.11), channel_id=1, replica_groups=mesh['blk'=64,'group'=8] {'group'}, use_global_device_ids=true, to_apply=%region_1.0 | all-reduce | flops 768 | bytes 6144 | tf_op jit(solution)/shard_map/pmax | solution.py:44
  82.3 0.0 copy-start.1
  82.3 0.2 exponential_reduce_fusion.1
  82.5 0.3 exponential_reduce_fusion
  82.8 1.9 collective-permute-start.2
  84.8 1.9 collective-permute-start.4
  86.7 63.1 %all-gather.1 = f32[8,1,768]{2,1,0:T(1,128)S(1)} all-gather(f32[1,1,768]{2,1,0:T(1,128)S(1)} %reshape.20), channel_id=2, replica_groups=mesh['blk'=64,'group'=8] {'group'}, dimensions={0}, use_global_device_ids=true | all-gather | bytes 27648 | tf_op jit(solution)/shard_map/all_gather | solution.py:46
  149.9 0.0 collective-permute-done.2
  149.9 0.0 collective-permute-done.4
  149.9 1.9 collective-permute-start.5
  151.8 1.9 collective-permute-start.3
  153.8 0.1 dynamic-slice_bitcast_fusion
  153.8 1.3 gather_fusion
  155.1 7.2 %collective-permute-done.5 = f32[96]{0:T(128)S(1)} collective-permute-done((f32[96]{0:T(128)S(1)}, f32[96]{0:T(128)S(1)}, u32[]{:S(2)}, u32[]{:S(2)}) %collective-permute-start.5) | collective-permute-done | bytes 416 | tf_op jit(solution)/shard_map/ppermute | solution.py:13
  162.3 1.9 collective-permute-done.3
  164.2 0.6 fusion.24
  164.8 2.1 collective-permute-start.6
  166.9 1.3 collective-permute-done.6
  168.2 11.1 %collective-permute-start.7 = (f32[96]{0:T(128)S(1)}, f32[96]{0:T(128)S(1)}, u32[]{:S(2)}, u32[]{:S(2)}) collective-permute-start(f32[96]{0:T(128)S(1)} %collective-permute-done.6), channel_id=1, source_target_pairs={{0,504},{8,0},{16,8},{24,16},{32,24},{40,32},{48,40},{56,48},{64,5... | collective-permute-start | bytes 1160 | tf_op jit(solution)/shard_map/ppermute | solution.py:13
  179.3 1.3 collective-permute-done.7
  180.6 0.0 copy-done.1
  180.6 4.2 %bitcast_multiply_fusion = f32[768,512]{1,0:T(8,128)} fusion(f32[1,96,512]{2,1,0:T(8,128)S(1)} %bitcast.90, f32[1,96,512]{2,1,0:T(8,128)S(1)} %bitcast.88, f32[1,96,512]{2,1,0:T(8,128)S(1)} %bitcast.86, s32[96]{0:T(128)S(1)} %iota_add_fusion, f32[3,96]{1,0:T(4,128)S(1)} %pad_maximum_fusion.3, f32[768]{0:T(1024)S(1)} %log_add_fusion, ...), kind=kOutput, calls=%fused_computation.1 | convolution fusion | flops 1361412096 | bytes 3052035 | tf_op jit(solution)/shard_map/rkc,kcd->rd/dot_general | solution.py:83
  184.7 0.0 reduce-scatter.2.cloned.1.call-update
  184.8 2.0 fusion.7
  186.8 1.9 collective-permute-start.8
  188.7 12.6 %collective-permute-done.8 = f32[96,512]{1,0:T(8,128)S(1)} collective-permute-done((f32[96,512]{1,0:T(8,128)S(1)}, f32[96,512]{1,0:T(8,128)S(1)}, u32[]{:S(2)}, u32[]{:S(2)}) %collective-permute-start.8) | collective-permute-done | bytes 196640 | tf_op jit(solution)/shard_map/ppermute | solution.py:13
  201.3 1.9 collective-permute-start.9
  203.2 20.6 %collective-permute-done.9 = f32[96,512]{1,0:T(8,128)S(1)} collective-permute-done((f32[96,512]{1,0:T(8,128)S(1)}, f32[96,512]{1,0:T(8,128)S(1)}, u32[]{:S(2)}, u32[]{:S(2)}) %collective-permute-start.9) | collective-permute-done | bytes 196640 | tf_op jit(solution)/shard_map/ppermute | solution.py:13
  223.8 0.7 fusion.11
  224.5 93.3 %reduce-scatter.2.cloned.1.call-done = f32[96,512]{1,0:T(8,128)} async-done(((f32[768,512]{1,0:T(8,128)}), f32[96,512]{1,0:T(8,128)}) %reduce-scatter.2.cloned.1.call-update) | async-done | bytes 196624 | tf_op jit(solution)/shard_map/reduce_scatter | solution.py:82
  (13 shorter events, 0.2 us)
Async XLA Ops:
  7.2 30.7 %copy-start = (f32[768,512]{1,0:T(8,128)S(1)}, f32[768,512]{1,0:T(8,128)}, u32[]{:S(2)}) copy-start(f32[768,512]{1,0:T(8,128)} %param.2) | copy-start | bytes 4718596
  7.2 310.6 %reduce-scatter.2.cloned.1.call-start = ((), (), s32[]{:S(2)}) async-start(), calls=%async_computation.1 | async-start | bytes 1769472 | tf_op jit(solution)/shard_map/reduce_scatter | solution.py:82
  7.2 16.1 %collective-permute-start = (f32[96,512]{1,0:T(8,128)}, f32[96,512]{1,0:T(8,128)S(1)}, u32[]{:S(2)}, u32[]{:S(2)}) collective-permute-start(f32[96,512]{1,0:T(8,128)} %param.3), channel_id=1, source_target_pairs={{0,504},{8,0},{16,8},{24,16},{32,24},{40,32},{48,40},{56,48},{64,5... | collective-permute-start | bytes 589832 | tf_op jit(solution)/shard_map/ppermute | solution.py:13
  23.3 14.5 %collective-permute-start.1 = (f32[96,512]{1,0:T(8,128)S(1)}, f32[96,512]{1,0:T(8,128)S(1)}, u32[]{:S(2)}, u32[]{:S(2)}) collective-permute-start(f32[96,512]{1,0:T(8,128)S(1)} %collective-permute-done), channel_id=1, source_target_pairs={{0,504},{8,0},{16,8},{24,16},{32,24},{40,32},{48,40},{56,48},{64,5... | collective-permute-start | bytes 589832 | tf_op jit(solution)/shard_map/ppermute | solution.py:13
  82.3 98.3 %copy-start.1 = (f32[96,512]{1,0:T(8,128)S(1)}, f32[96,512]{1,0:T(8,128)}, u32[]{:S(2)}) copy-start(f32[96,512]{1,0:T(8,128)} %param.3) | copy-start | bytes 589828
  82.8 67.0 %collective-permute-start.2 = (f32[96]{0:T(128)S(1)}, f32[96]{0:T(128)S(1)}, u32[]{:S(2)}, u32[]{:S(2)}) collective-permute-start(f32[96]{0:T(128)S(1)} %slice_bitcast_fusion.4), channel_id=1, source_target_pairs={{0,8},{8,16},{16,24},{24,32},{32,40},{40,48},{48,56},{56,64},{64,7... | collective-permute-start | bytes 1160 | tf_op jit(solution)/shard_map/ppermute | solution.py:13
  84.8 65.1 %collective-permute-start.4 = (f32[96]{0:T(128)S(1)}, f32[96]{0:T(128)S(1)}, u32[]{:S(2)}, u32[]{:S(2)}) collective-permute-start(f32[96]{0:T(128)S(1)} %slice_bitcast_fusion.3), channel_id=1, source_target_pairs={{0,8},{8,16},{16,24},{24,32},{32,40},{40,48},{48,56},{56,64},{64,7... | collective-permute-start | bytes 1160 | tf_op jit(solution)/shard_map/ppermute | solution.py:13
  149.9 12.4 %collective-permute-start.5 = (f32[96]{0:T(128)S(1)}, f32[96]{0:T(128)S(1)}, u32[]{:S(2)}, u32[]{:S(2)}) collective-permute-start(f32[96]{0:T(128)S(1)} %get-tuple-element.9), channel_id=1, source_target_pairs={{0,8},{8,16},{16,24},{24,32},{32,40},{40,48},{48,56},{56,64},{64,7... | collective-permute-start | bytes 1160 | tf_op jit(solution)/shard_map/ppermute | solution.py:13
  151.8 12.4 %collective-permute-start.3 = (f32[96]{0:T(128)S(1)}, f32[96]{0:T(128)S(1)}, u32[]{:S(2)}, u32[]{:S(2)}) collective-permute-start(f32[96]{0:T(128)S(1)} %get-tuple-element.8), channel_id=1, source_target_pairs={{0,8},{8,16},{16,24},{24,32},{32,40},{40,48},{48,56},{56,64},{64,7... | collective-permute-start | bytes 1160 | tf_op jit(solution)/shard_map/ppermute | solution.py:13
  164.8 3.4 %collective-permute-start.6 = (f32[96]{0:T(128)S(1)}, f32[96]{0:T(128)S(1)}, u32[]{:S(2)}, u32[]{:S(2)}) collective-permute-start(f32[96]{0:T(128)S(1)} %get-tuple-element.7), channel_id=1, source_target_pairs={{0,504},{8,0},{16,8},{24,16},{32,24},{40,32},{48,40},{56,48},{64,5... | collective-permute-start | bytes 1160 | tf_op jit(solution)/shard_map/ppermute | solution.py:13
  168.2 12.4 %collective-permute-start.7 = (f32[96]{0:T(128)S(1)}, f32[96]{0:T(128)S(1)}, u32[]{:S(2)}, u32[]{:S(2)}) collective-permute-start(f32[96]{0:T(128)S(1)} %collective-permute-done.6), channel_id=1, source_target_pairs={{0,504},{8,0},{16,8},{24,16},{32,24},{40,32},{48,40},{56,48},{64,5... | collective-permute-start | bytes 1160 | tf_op jit(solution)/shard_map/ppermute | solution.py:13
  186.8 14.5 %collective-permute-start.8 = (f32[96,512]{1,0:T(8,128)S(1)}, f32[96,512]{1,0:T(8,128)S(1)}, u32[]{:S(2)}, u32[]{:S(2)}) collective-permute-start(f32[96,512]{1,0:T(8,128)S(1)} %slice_bitcast_fusion.2), channel_id=1, source_target_pairs={{0,8},{8,16},{16,24},{24,32},{32,40},{40,48},{48,56},{56,64},{64,7... | collective-permute-start | bytes 589832 | tf_op jit(solution)/shard_map/ppermute | solution.py:13
  201.3 22.5 %collective-permute-start.9 = (f32[96,512]{1,0:T(8,128)S(1)}, f32[96,512]{1,0:T(8,128)S(1)}, u32[]{:S(2)}, u32[]{:S(2)}) collective-permute-start(f32[96,512]{1,0:T(8,128)S(1)} %fusion.12), channel_id=1, source_target_pairs={{0,8},{8,16},{16,24},{24,32},{32,40},{40,48},{48,56},{56,64},{64,7... | collective-permute-start | bytes 589832 | tf_op jit(solution)/shard_map/ppermute | solution.py:13
Sparse Core Ops, SparseCore 0:
  184.9 132.8 reduce-scatter.1
